TPU v7x, 512 devices: a whole 4x8x8 slice. The times are simulated.
512 devices in a mesh: lon: 32 (over z, x), lat: 16 (over y, core).
Axes of the slice: x: 4, y: 8, z: 8, core: 2. Of those that a mesh axis runs over, the one named last changes fastest.
Arguments:
- right_side: float32 [2, 32, 256, 4096], P(None, None, 'lat', 'lon'), may hold values from -36 to 36
- sea_mask: int32 [32, 256, 4096], P(None, 'lat', 'lon'), may hold values 0 or 1
- levels: int32 [256, 4096], P('lat', 'lon'), may hold values from 0 to 32
- east_diffusivity: bfloat16 [32, 256, 4096], P(None, 'lat', 'lon'), may hold values from 1 to 8
- north_diffusivity: bfloat16 [32, 256, 4096], P(None, 'lat', 'lon'), may hold values from 1 to 8
- vertical_diffusivity: bfloat16 [32, 256, 4096], P(None, 'lat', 'lon'), may hold values from 0.5 to 8
Outputs:
- solution_field: float32 [2, 32, 256, 4096], P(None, None, 'lat', 'lon')
- residual: float32 [2, 32, 256, 4096], P(None, None, 'lat', 'lon')
All inputs are finite; a program needn't handle non-finite values. No bound on the sum of `sea_mask` on one device may be relied on, other than what follows from the above.
Results may differ from a plain program's by a relative error of at most 0.004.
Values sent between devices are 32-bit elements; how exact they have to be, the bound alone decides.
A program may use at most 64 MiB of HBM per device.

v0:
```python
import jax
import jax.numpy as jnp
from jax import lax
from jax.sharding import PartitionSpec as P

ITERS = 2


def from_behind(x, axis, by):
    devices = lax.axis_size(axis)
    return lax.ppermute(x, axis, [(i, (i + by) % devices) for i in range(devices)])


def shifted(x, axis, by):
    devices = lax.axis_size(axis)
    pairs = [(i, i + by) for i in range(devices) if 0 <= i + by < devices]
    return lax.ppermute(x, axis, pairs)


def local_sum(first, second):
    return jnp.sum(first * second, axis=(1, 2, 3))


def expand(scalars):
    return scalars[:, None, None, None]


def vertical_change(field, coef_down):
    value_below = jnp.concatenate([field[:, 1:], jnp.zeros_like(field[:, :1])], axis=1)
    flux_down = coef_down * (value_below - field)
    flux_above = jnp.concatenate([jnp.zeros_like(flux_down[:, :1]), flux_down[:, :-1]], axis=1)
    return flux_above - flux_down


def body(right_side, sea_mask, levels, east_diffusivity, north_diffusivity, vertical_diffusivity):
    depth_index = lax.broadcasted_iota(jnp.int32, sea_mask.shape, 0)
    ocean_flag = ((sea_mask == 1) & (depth_index < levels[None])).astype(jnp.int32)
    east_column = from_behind(ocean_flag[:, :, :1], "lon", -1)
    north_row = shifted(ocean_flag[:, :1, :], "lat", -1)
    ocean = ocean_flag.astype(jnp.float32)
    ocean_east = jnp.concatenate([ocean[:, :, 1:], east_column.astype(jnp.float32)], axis=2)
    ocean_north = jnp.concatenate([ocean[:, 1:, :], north_row.astype(jnp.float32)], axis=1)
    ocean_below = jnp.concatenate([ocean[1:], jnp.zeros_like(ocean[:1])], axis=0)
    coef_east = east_diffusivity.astype(jnp.float32) * ocean * ocean_east
    coef_north = north_diffusivity.astype(jnp.float32) * ocean * ocean_north
    coef_down = vertical_diffusivity.astype(jnp.float32) * ocean * ocean_below
    solution = jnp.zeros_like(right_side)
    residual = right_side

    def sum_squares(field):
        return lax.psum(local_sum(field, field), ("lon", "lat"))

    direction = right_side
    norm_now = sum_squares(residual)
    for iteration in range(ITERS):
        first_column = from_behind(direction[:, :, :, :1], "lon", -1)
        first_row = shifted(direction[:, :, :1, :], "lat", -1)
        value_east = jnp.concatenate([direction[:, :, :, 1:], first_column], axis=3)
        value_north = jnp.concatenate([direction[:, :, 1:, :], first_row], axis=2)
        flux_east = coef_east * (value_east - direction)
        flux_north = coef_north * (value_north - direction)
        last_column = from_behind(flux_east[:, :, :, -1:], "lon", 1)
        last_row = shifted(flux_north[:, :, -1:, :], "lat", 1)
        flux_west = jnp.concatenate([last_column, flux_east[:, :, :, :-1]], axis=3)
        flux_south = jnp.concatenate([last_row, flux_north[:, :, :-1, :]], axis=2)
        image = (
            direction
            + (flux_west - flux_east)
            + (flux_south - flux_north)
            + vertical_change(direction, coef_down)
        )
        step_size = norm_now / lax.psum(local_sum(direction, image), ("lon", "lat"))
        solution = solution + expand(step_size) * direction
        residual = residual - expand(step_size) * image
        norm_next = sum_squares(residual)
        direction = residual + expand(norm_next / norm_now) * direction
        norm_now = norm_next
    return (solution, residual)


def solution(mesh):
    return jax.shard_map(
        body,
        mesh=mesh,
        in_specs=(
            P(None, None, "lat", "lon"),
            P(None, "lat", "lon"),
            P("lat", "lon"),
            P(None, "lat", "lon"),
            P(None, "lat", "lon"),
            P(None, "lat", "lon"),
        ),
        out_specs=(P(None, None, "lat", "lon"), P(None, None, "lat", "lon")),
        check_vma=False,
    )
```

profile of v0, /device:TPU:1, one launch (start us, length us, event | category | flops | bytes accessed | tf_op | source)
XLA Modules:
  0.0 386.5 jit_solution(15036093700359671659)
XLA Ops:
  0.6 1.1 fusion.14
  1.7 8.8 %collective-permute-start.3 = (s32[32,1,128]{2,1,0:T(1,128)S(1)}, s32[32,1,128]{2,1,0:T(1,128)S(1)}, u32[]{:S(2)}, u32[]{:S(2)}) collective-permute-start(s32[32,1,128]{2,1,0:T(1,128)S(1)} %slice.105), channel_id=1, source_target_pairs={{1,0},{2,1},{3,2},{4,3},{5,4},{6,5},{7,6},{8,7},{9,8},{10,9},{11,1... | collective-permute-start | bytes 49160 | tf_op jit(solution)/shard_map/ppermute | solution.py:17
  10.5 7.5 %collective-permute-start = (s32[32,16,1]{2,1,0:T(8,128)S(1)}, s32[32,16,1]{2,1,0:T(8,128)S(1)}, u32[]{:S(2)}, u32[]{:S(2)}) collective-permute-start(s32[32,16,1]{2,1,0:T(8,128)S(1)} %bitcast.13), channel_id=1, source_target_pairs={{0,496},{16,0},{32,16},{48,32},{64,48},{80,64},{96,80},{112,96},{1... | collective-permute-start | bytes 6152 | tf_op jit(solution)/shard_map/ppermute | solution.py:11
  18.1 1.9 collective-permute-start.4
  20.0 2.5 collective-permute-start.1
  22.6 0.2 slice.77
  22.8 0.1 slice.100
  23.0 1.2 collective-permute-done
  24.2 0.2 maximum_multiply_fusion
  24.4 10.9 %collective-permute-done.1 = f32[2,32,16,1]{3,2,1,0:T(8,128)S(1)} collective-permute-done((f32[2,32,16,1]{3,2,1,0:T(8,128)S(1)}, f32[2,32,16,1]{3,2,1,0:T(8,128)S(1)}, u32[]{:S(2)}, u32[]{:S(2)}) %collective-permute-start.1) | collective-permute-done | bytes 4128 | tf_op jit(solution)/shard_map/ppermute | solution.py:11
  35.3 0.4 fusion
  35.7 4.3 %collective-permute-start.5 = (f32[2,32,1,128]{3,2,1,0:T(1,128)S(1)}, f32[2,32,1,128]{3,2,1,0:T(1,128)S(1)}, u32[]{:S(2)}, u32[]{:S(2)}) collective-permute-start(f32[2,32,1,128]{3,2,1,0:T(1,128)S(1)} %slice.106), channel_id=1, source_target_pairs={{0,1},{1,2},{2,3},{3,4},{4,5},{5,6},{6,7},{7,8},{8,9},{9,10},{10,1... | collective-permute-start | bytes 98312 | tf_op jit(solution)/shard_map/ppermute | solution.py:17
  40.0 0.2 slice.102
  40.2 1.9 collective-permute-start.2
  42.2 15.7 %collective-permute-done.2 = f32[2,32,16,1]{3,2,1,0:T(8,128)S(1)} collective-permute-done((f32[2,32,16,1]{3,2,1,0:T(8,128)S(1)}, f32[2,32,16,1]{3,2,1,0:T(8,128)S(1)}, u32[]{:S(2)}, u32[]{:S(2)}) %collective-permute-start.2) | collective-permute-done | bytes 4128 | tf_op jit(solution)/shard_map/ppermute | solution.py:11
  57.9 0.5 multiply_reduce_fusion.2
  58.4 97.2 %all-reduce.5 = (f32[2]{0:T(128)S(1)}, f32[2]{0:T(128)S(1)}) all-reduce(f32[2]{0:T(128)S(1)} %get-tuple-element.3, f32[2]{0:T(128)S(1)} %get-tuple-element.2), channel_id=1, replica_groups=mesh['lon'=32,'lat'=16] {'lon','lat'}, use_global_device_ids=true, to_apply=%region_1.0 | all-reduce | flops 4 | bytes 32 | tf_op jit(solution)/shard_map/psum | solution.py:51
  155.6 0.3 multiply_reduce_fusion.1
  155.9 94.4 %psum.30 = f32[2]{0:T(128)S(1)} all-reduce(f32[2]{0:T(128)S(1)} %multiply_reduce_fusion.1), channel_id=1, replica_groups=mesh['lon'=32,'lat'=16] {'lon','lat'}, use_global_device_ids=true, to_apply=%region_5.0 | all-reduce | flops 2 | bytes 16 | tf_op jit(solution)/shard_map/psum | solution.py:51
  250.3 0.1 multiply_add_fusion.1
  250.5 2.6 collective-permute-start.8
  253.1 4.5 %collective-permute-start.6 = (f32[2,32,16,1]{3,2,1,0:T(8,128)S(1)}, f32[2,32,16,1]{3,2,1,0:T(8,128)S(1)}, u32[]{:S(2)}, u32[]{:S(2)}) collective-permute-start(f32[2,32,16,1]{3,2,1,0:T(8,128)S(1)} %bitcast.8), channel_id=1, source_target_pairs={{0,496},{16,0},{32,16},{48,32},{64,48},{80,64},{96,80},{112,96},{1... | collective-permute-start | bytes 12296 | tf_op jit(solution)/shard_map/ppermute | solution.py:11
  257.7 0.2 slice.110
  257.9 11.3 %collective-permute-done.6 = f32[2,32,16,1]{3,2,1,0:T(8,128)S(1)} collective-permute-done((f32[2,32,16,1]{3,2,1,0:T(8,128)S(1)}, f32[2,32,16,1]{3,2,1,0:T(8,128)S(1)}, u32[]{:S(2)}, u32[]{:S(2)}) %collective-permute-start.6) | collective-permute-done | bytes 4128 | tf_op jit(solution)/shard_map/ppermute | solution.py:11
  269.2 0.4 fusion.5
  269.6 2.6 collective-permute-start.9
  272.2 0.2 slice.112
  272.4 2.8 collective-permute-start.7
  275.3 15.8 %collective-permute-done.7 = f32[2,32,16,1]{3,2,1,0:T(8,128)S(1)} collective-permute-done((f32[2,32,16,1]{3,2,1,0:T(8,128)S(1)}, f32[2,32,16,1]{3,2,1,0:T(8,128)S(1)}, u32[]{:S(2)}, u32[]{:S(2)}) %collective-permute-start.7) | collective-permute-done | bytes 4128 | tf_op jit(solution)/shard_map/ppermute | solution.py:11
  291.1 0.5 multiply_reduce_fusion
  291.6 93.8 %psum.31 = f32[2]{0:T(128)S(1)} all-reduce(f32[2]{0:T(128)S(1)} %get-tuple-element.6), channel_id=1, replica_groups=mesh['lon'=32,'lat'=16] {'lon','lat'}, use_global_device_ids=true, to_apply=%region_7.0 | all-reduce | flops 2 | bytes 16 | tf_op jit(solution)/shard_map/psum | solution.py:72
  385.3 1.2 multiply_subtract_fusion
  (31 shorter events, 0.5 us)
Async XLA Ops:
  0.6 17.4 %copy-start = (f32[2,32,16,128]{3,2,1,0:T(8,128)S(1)}, f32[2,32,16,128]{3,2,1,0:T(8,128)}, u32[]{:S(2)}) copy-start(f32[2,32,16,128]{3,2,1,0:T(8,128)} %param.6) | copy-start | bytes 1572868
  1.7 22.4 %collective-permute-start.3 = (s32[32,1,128]{2,1,0:T(1,128)S(1)}, s32[32,1,128]{2,1,0:T(1,128)S(1)}, u32[]{:S(2)}, u32[]{:S(2)}) collective-permute-start(s32[32,1,128]{2,1,0:T(1,128)S(1)} %slice.105), channel_id=1, source_target_pairs={{1,0},{2,1},{3,2},{4,3},{5,4},{6,5},{7,6},{8,7},{9,8},{10,9},{11,1... | collective-permute-start | bytes 49160 | tf_op jit(solution)/shard_map/ppermute | solution.py:17
  10.5 13.6 %collective-permute-start = (s32[32,16,1]{2,1,0:T(8,128)S(1)}, s32[32,16,1]{2,1,0:T(8,128)S(1)}, u32[]{:S(2)}, u32[]{:S(2)}) collective-permute-start(s32[32,16,1]{2,1,0:T(8,128)S(1)} %bitcast.13), channel_id=1, source_target_pairs={{0,496},{16,0},{32,16},{48,32},{64,48},{80,64},{96,80},{112,96},{1... | collective-permute-start | bytes 6152 | tf_op jit(solution)/shard_map/ppermute | solution.py:11
  18.1 17.2 %collective-permute-start.4 = (f32[2,32,1,128]{3,2,1,0:T(1,128)S(1)}, f32[2,32,1,128]{3,2,1,0:T(1,128)S(1)}, u32[]{:S(2)}, u32[]{:S(2)}) collective-permute-start(f32[2,32,1,128]{3,2,1,0:T(1,128)S(1)} %slice.84), channel_id=1, source_target_pairs={{1,0},{2,1},{3,2},{4,3},{5,4},{6,5},{7,6},{8,7},{9,8},{10,9},{11,1... | collective-permute-start | bytes 98312 | tf_op jit(solution)/shard_map/ppermute | solution.py:17
  20.0 15.3 %collective-permute-start.1 = (f32[2,32,16,1]{3,2,1,0:T(8,128)S(1)}, f32[2,32,16,1]{3,2,1,0:T(8,128)S(1)}, u32[]{:S(2)}, u32[]{:S(2)}) collective-permute-start(f32[2,32,16,1]{3,2,1,0:T(8,128)S(1)} %bitcast.7), channel_id=1, source_target_pairs={{0,496},{16,0},{32,16},{48,32},{64,48},{80,64},{96,80},{112,96},{1... | collective-permute-start | bytes 12296 | tf_op jit(solution)/shard_map/ppermute | solution.py:11
  22.9 1.2 copy-start.1
  23.0 1.2 copy-start.2
  23.0 1.2 copy-start.3
  35.7 22.2 %collective-permute-start.5 = (f32[2,32,1,128]{3,2,1,0:T(1,128)S(1)}, f32[2,32,1,128]{3,2,1,0:T(1,128)S(1)}, u32[]{:S(2)}, u32[]{:S(2)}) collective-permute-start(f32[2,32,1,128]{3,2,1,0:T(1,128)S(1)} %slice.106), channel_id=1, source_target_pairs={{0,1},{1,2},{2,3},{3,4},{4,5},{5,6},{6,7},{7,8},{8,9},{9,10},{10,1... | collective-permute-start | bytes 98312 | tf_op jit(solution)/shard_map/ppermute | solution.py:17
  40.2 17.7 %collective-permute-start.2 = (f32[2,32,16,1]{3,2,1,0:T(8,128)S(1)}, f32[2,32,16,1]{3,2,1,0:T(8,128)S(1)}, u32[]{:S(2)}, u32[]{:S(2)}) collective-permute-start(f32[2,32,16,1]{3,2,1,0:T(8,128)S(1)} %slice.102), channel_id=1, source_target_pairs={{0,16},{16,32},{32,48},{48,64},{64,80},{80,96},{96,112},{112,128},... | collective-permute-start | bytes 12296 | tf_op jit(solution)/shard_map/ppermute | solution.py:11
  250.5 18.8 %collective-permute-start.8 = (f32[2,32,1,128]{3,2,1,0:T(1,128)S(1)}, f32[2,32,1,128]{3,2,1,0:T(1,128)S(1)}, u32[]{:S(2)}, u32[]{:S(2)}) collective-permute-start(f32[2,32,1,128]{3,2,1,0:T(1,128)S(1)} %slice.115), channel_id=1, source_target_pairs={{1,0},{2,1},{3,2},{4,3},{5,4},{6,5},{7,6},{8,7},{9,8},{10,9},{11,1... | collective-permute-start | bytes 98312 | tf_op jit(solution)/shard_map/ppermute | solution.py:17
  253.1 16.2 %collective-permute-start.6 = (f32[2,32,16,1]{3,2,1,0:T(8,128)S(1)}, f32[2,32,16,1]{3,2,1,0:T(8,128)S(1)}, u32[]{:S(2)}, u32[]{:S(2)}) collective-permute-start(f32[2,32,16,1]{3,2,1,0:T(8,128)S(1)} %bitcast.8), channel_id=1, source_target_pairs={{0,496},{16,0},{32,16},{48,32},{64,48},{80,64},{96,80},{112,96},{1... | collective-permute-start | bytes 12296 | tf_op jit(solution)/shard_map/ppermute | solution.py:11
  269.6 21.5 %collective-permute-start.9 = (f32[2,32,1,128]{3,2,1,0:T(1,128)S(1)}, f32[2,32,1,128]{3,2,1,0:T(1,128)S(1)}, u32[]{:S(2)}, u32[]{:S(2)}) collective-permute-start(f32[2,32,1,128]{3,2,1,0:T(1,128)S(1)} %slice.116), channel_id=1, source_target_pairs={{0,1},{1,2},{2,3},{3,4},{4,5},{5,6},{6,7},{7,8},{8,9},{9,10},{10,1... | collective-permute-start | bytes 98312 | tf_op jit(solution)/shard_map/ppermute | solution.py:17
  272.4 18.7 %collective-permute-start.7 = (f32[2,32,16,1]{3,2,1,0:T(8,128)S(1)}, f32[2,32,16,1]{3,2,1,0:T(8,128)S(1)}, u32[]{:S(2)}, u32[]{:S(2)}) collective-permute-start(f32[2,32,16,1]{3,2,1,0:T(8,128)S(1)} %slice.112), channel_id=1, source_target_pairs={{0,16},{16,32},{32,48},{48,64},{64,80},{80,96},{96,112},{112,128},... | collective-permute-start | bytes 12296 | tf_op jit(solution)/shard_map/ppermute | solution.py:11
where the time goes:
time: 387 us
  blocking collectives  285 us (74%)
  waiting for transfers between devices  54.9 us (14%)
  starting transfers between devices  39.4 us (10%)
  other arithmetic  4.62 us (1%)
    psum x2, blocking collectives, sum_squares(): return lax.psum(local_sum(field, field), ('lon', 'lat'))  192 us
    psum x1, blocking collectives, body(): step_size = norm_now / lax.psum(local_sum(direction, image), ('lon', 'lat'))  93.8 us
    ppermute x5, waiting for transfers between devices, from_behind(): lax.ppermute(x, axis, [(i, (i + by) % devices) for i in range(devices)])  54.9 us
    ppermute x5, starting transfers between devices, shifted(): return lax.ppermute(x, axis, pairs)  20.2 us
    ppermute x5, starting transfers between devices, from_behind(): lax.ppermute(x, axis, [(i, (i + by) % devices) for i in range(devices)])  19.2 us
  transfers between devices with their start and end apart: 10, of which 5 were waited for; matrix products, arithmetic and copies ran while one was open for 0% of the time, Pallas kernels for 0%

commit v1 on v0

--- a/solution.py
+++ b/solution.py
@@ -48,7 +48,7 @@
     residual = right_side
 
     def sum_squares(field):
-        return lax.psum(local_sum(field, field), ("lon", "lat"))
+        return jnp.sum(lax.all_gather(local_sum(field, field), ("lon", "lat")), axis=0)
 
     direction = right_side
     norm_now = sum_squares(residual)

time: 387 us -> 389 us (level)
    unnamed x0 -> x2, blocking collectives: none -> 192 us
    psum x2 -> x0, blocking collectives: 192 us -> none  [sum_squares(): return lax.psum(local_sum(field, field), ('lon', 'lat'))]
where the time goes in v1:
time: 389 us
  blocking collectives  285 us (73%)
  waiting for transfers between devices  55 us (14%)
  starting transfers between devices  39.4 us (10%)
  other arithmetic  5.76 us (1%)
    unnamed x2, blocking collectives  192 us
    psum x1, blocking collectives, body(): step_size = norm_now / lax.psum(local_sum(direction, image), ('lon', 'lat'))  93.8 us
    ppermute x5, waiting for transfers between devices, from_behind(): lax.ppermute(x, axis, [(i, (i + by) % devices) for i in range(devices)])  55 us
    ppermute x5, starting transfers between devices, shifted(): return lax.ppermute(x, axis, pairs)  20.2 us
    ppermute x5, starting transfers between devices, from_behind(): lax.ppermute(x, axis, [(i, (i + by) % devices) for i in range(devices)])  19.2 us
  transfers between devices with their start and end apart: 10, of which 5 were waited for; matrix products, arithmetic and copies ran while one was open for 0% of the time, Pallas kernels for 0%

profile of v1, /device:TPU:1, one launch (start us, length us, event | category | flops | bytes accessed | tf_op | source)
XLA Modules:
  0.0 388.7 jit_solution(4771734816059415103)
XLA Ops:
  0.6 1.1 fusion.14
  1.7 8.8 %collective-permute-start.3 = (s32[32,1,128]{2,1,0:T(1,128)S(1)}, s32[32,1,128]{2,1,0:T(1,128)S(1)}, u32[]{:S(2)}, u32[]{:S(2)}) collective-permute-start(s32[32,1,128]{2,1,0:T(1,128)S(1)} %slice.105), channel_id=1, source_target_pairs={{1,0},{2,1},{3,2},{4,3},{5,4},{6,5},{7,6},{8,7},{9,8},{10,9},{11,1... | collective-permute-start | bytes 49160 | tf_op jit(solution)/shard_map/ppermute | solution.py:17
  10.5 7.5 %collective-permute-start = (s32[32,16,1]{2,1,0:T(8,128)S(1)}, s32[32,16,1]{2,1,0:T(8,128)S(1)}, u32[]{:S(2)}, u32[]{:S(2)}) collective-permute-start(s32[32,16,1]{2,1,0:T(8,128)S(1)} %bitcast.13), channel_id=1, source_target_pairs={{0,496},{16,0},{32,16},{48,32},{64,48},{80,64},{96,80},{112,96},{1... | collective-permute-start | bytes 6152 | tf_op jit(solution)/shard_map/ppermute | solution.py:11
  18.1 1.9 collective-permute-start.4
  20.0 2.5 collective-permute-start.1
  22.6 0.2 slice.77
  23.0 1.2 collective-permute-done
  24.4 10.9 %collective-permute-done.1 = f32[2,32,16,1]{3,2,1,0:T(8,128)S(1)} collective-permute-done((f32[2,32,16,1]{3,2,1,0:T(8,128)S(1)}, f32[2,32,16,1]{3,2,1,0:T(8,128)S(1)}, u32[]{:S(2)}, u32[]{:S(2)}) %collective-permute-start.1) | collective-permute-done | bytes 4128 | tf_op jit(solution)/shard_map/ppermute | solution.py:11
  35.3 0.4 fusion
  35.7 4.3 %collective-permute-start.5 = (f32[2,32,1,128]{3,2,1,0:T(1,128)S(1)}, f32[2,32,1,128]{3,2,1,0:T(1,128)S(1)}, u32[]{:S(2)}, u32[]{:S(2)}) collective-permute-start(f32[2,32,1,128]{3,2,1,0:T(1,128)S(1)} %slice.106), channel_id=1, source_target_pairs={{0,1},{1,2},{2,3},{3,4},{4,5},{5,6},{6,7},{7,8},{8,9},{9,10},{10,1... | collective-permute-start | bytes 98312 | tf_op jit(solution)/shard_map/ppermute | solution.py:17
  40.0 0.2 slice.102
  40.2 1.9 collective-permute-start.2
  42.2 15.8 %collective-permute-done.2 = f32[2,32,16,1]{3,2,1,0:T(8,128)} collective-permute-done((f32[2,32,16,1]{3,2,1,0:T(8,128)S(1)}, f32[2,32,16,1]{3,2,1,0:T(8,128)}, u32[]{:S(2)}, u32[]{:S(2)}) %collective-permute-start.2) | collective-permute-done | bytes 4128 | tf_op jit(solution)/shard_map/ppermute | solution.py:11
  58.0 1.5 multiply_reduce_fusion.2
  59.5 0.2 dynamic-update-slice
  59.8 97.2 %all-reduce.7 = (f32[1024]{0:T(1024)S(1)}, f32[2]{0:T(128)S(1)}) all-reduce(f32[1024]{0:T(1024)S(1)} %dynamic-update-slice, f32[2]{0:T(128)S(1)} %get-tuple-element.2), channel_id=2, replica_groups=mesh['lon'=32,'lat'=16] {'lon','lat'}, use_global_device_ids=true, to_apply=%add.5 | all-reduce | flops 1026 | bytes 8208
  157.0 0.2 reshape.15
  157.3 0.3 multiply_reduce_fusion.1
  157.7 94.4 %all-reduce.6 = f32[1024]{0:T(1024)S(1)} all-reduce(f32[1024]{0:T(1024)S(1)} %dynamic-update-slice.1), channel_id=3, replica_groups=mesh['lon'=32,'lat'=16] {'lon','lat'}, use_global_device_ids=true, to_apply=%add.6 | all-reduce | flops 1024 | bytes 8192
  252.1 0.2 reshape.16
  252.6 2.6 collective-permute-start.8
  255.2 4.5 %collective-permute-start.6 = (f32[2,32,16,1]{3,2,1,0:T(8,128)S(1)}, f32[2,32,16,1]{3,2,1,0:T(8,128)S(1)}, u32[]{:S(2)}, u32[]{:S(2)}) collective-permute-start(f32[2,32,16,1]{3,2,1,0:T(8,128)S(1)} %bitcast.8), channel_id=1, source_target_pairs={{0,496},{16,0},{32,16},{48,32},{64,48},{80,64},{96,80},{112,96},{1... | collective-permute-start | bytes 12296 | tf_op jit(solution)/shard_map/ppermute | solution.py:11
  259.8 0.2 slice.110
  260.0 11.3 %collective-permute-done.6 = f32[2,32,16,1]{3,2,1,0:T(8,128)S(1)} collective-permute-done((f32[2,32,16,1]{3,2,1,0:T(8,128)S(1)}, f32[2,32,16,1]{3,2,1,0:T(8,128)S(1)}, u32[]{:S(2)}, u32[]{:S(2)}) %collective-permute-start.6) | collective-permute-done | bytes 4128 | tf_op jit(solution)/shard_map/ppermute | solution.py:11
  271.4 0.3 fusion.5
  271.8 2.6 collective-permute-start.9
  274.3 0.2 slice.112
  274.5 2.8 collective-permute-start.7
  277.4 15.8 %collective-permute-done.7 = f32[2,32,16,1]{3,2,1,0:T(8,128)S(1)} collective-permute-done((f32[2,32,16,1]{3,2,1,0:T(8,128)S(1)}, f32[2,32,16,1]{3,2,1,0:T(8,128)S(1)}, u32[]{:S(2)}, u32[]{:S(2)}) %collective-permute-start.7) | collective-permute-done | bytes 4128 | tf_op jit(solution)/shard_map/ppermute | solution.py:11
  293.2 0.5 multiply_reduce_fusion
  293.7 93.8 %psum.15 = f32[2]{0:T(128)S(1)} all-reduce(f32[2]{0:T(128)S(1)} %get-tuple-element.6), channel_id=1, replica_groups=mesh['lon'=32,'lat'=16] {'lon','lat'}, use_global_device_ids=true, to_apply=%region_7.0 | all-reduce | flops 2 | bytes 16 | tf_op jit(solution)/shard_map/psum | solution.py:72
  387.5 1.2 multiply_subtract_fusion
  (39 shorter events, 1.3 us)
Async XLA Ops:
  0.6 17.4 %copy-start = (f32[2,32,16,128]{3,2,1,0:T(8,128)S(1)}, f32[2,32,16,128]{3,2,1,0:T(8,128)}, u32[]{:S(2)}) copy-start(f32[2,32,16,128]{3,2,1,0:T(8,128)} %param.6) | copy-start | bytes 1572868
  1.7 22.4 %collective-permute-start.3 = (s32[32,1,128]{2,1,0:T(1,128)S(1)}, s32[32,1,128]{2,1,0:T(1,128)S(1)}, u32[]{:S(2)}, u32[]{:S(2)}) collective-permute-start(s32[32,1,128]{2,1,0:T(1,128)S(1)} %slice.105), channel_id=1, source_target_pairs={{1,0},{2,1},{3,2},{4,3},{5,4},{6,5},{7,6},{8,7},{9,8},{10,9},{11,1... | collective-permute-start | bytes 49160 | tf_op jit(solution)/shard_map/ppermute | solution.py:17
  10.5 13.6 %collective-permute-start = (s32[32,16,1]{2,1,0:T(8,128)S(1)}, s32[32,16,1]{2,1,0:T(8,128)S(1)}, u32[]{:S(2)}, u32[]{:S(2)}) collective-permute-start(s32[32,16,1]{2,1,0:T(8,128)S(1)} %bitcast.13), channel_id=1, source_target_pairs={{0,496},{16,0},{32,16},{48,32},{64,48},{80,64},{96,80},{112,96},{1... | collective-permute-start | bytes 6152 | tf_op jit(solution)/shard_map/ppermute | solution.py:11
  18.1 17.2 %collective-permute-start.4 = (f32[2,32,1,128]{3,2,1,0:T(1,128)S(1)}, f32[2,32,1,128]{3,2,1,0:T(1,128)S(1)}, u32[]{:S(2)}, u32[]{:S(2)}) collective-permute-start(f32[2,32,1,128]{3,2,1,0:T(1,128)S(1)} %slice.84), channel_id=1, source_target_pairs={{1,0},{2,1},{3,2},{4,3},{5,4},{6,5},{7,6},{8,7},{9,8},{10,9},{11,1... | collective-permute-start | bytes 98312 | tf_op jit(solution)/shard_map/ppermute | solution.py:17
  20.0 15.3 %collective-permute-start.1 = (f32[2,32,16,1]{3,2,1,0:T(8,128)S(1)}, f32[2,32,16,1]{3,2,1,0:T(8,128)S(1)}, u32[]{:S(2)}, u32[]{:S(2)}) collective-permute-start(f32[2,32,16,1]{3,2,1,0:T(8,128)S(1)} %bitcast.7), channel_id=1, source_target_pairs={{0,496},{16,0},{32,16},{48,32},{64,48},{80,64},{96,80},{112,96},{1... | collective-permute-start | bytes 12296 | tf_op jit(solution)/shard_map/ppermute | solution.py:11
  22.9 1.2 copy-start.1
  23.0 1.2 copy-start.2
  23.0 1.2 copy-start.3
  35.7 22.3 %collective-permute-start.5 = (f32[2,32,1,128]{3,2,1,0:T(1,128)S(1)}, f32[2,32,1,128]{3,2,1,0:T(1,128)S(1)}, u32[]{:S(2)}, u32[]{:S(2)}) collective-permute-start(f32[2,32,1,128]{3,2,1,0:T(1,128)S(1)} %slice.106), channel_id=1, source_target_pairs={{0,1},{1,2},{2,3},{3,4},{4,5},{5,6},{6,7},{7,8},{8,9},{9,10},{10,1... | collective-permute-start | bytes 98312 | tf_op jit(solution)/shard_map/ppermute | solution.py:17
  40.2 17.8 %collective-permute-start.2 = (f32[2,32,16,1]{3,2,1,0:T(8,128)S(1)}, f32[2,32,16,1]{3,2,1,0:T(8,128)}, u32[]{:S(2)}, u32[]{:S(2)}) collective-permute-start(f32[2,32,16,1]{3,2,1,0:T(8,128)S(1)} %slice.102), channel_id=1, source_target_pairs={{0,16},{16,32},{32,48},{48,64},{64,80},{80,96},{96,112},{112,128},... | collective-permute-start | bytes 12296 | tf_op jit(solution)/shard_map/ppermute | solution.py:11
  252.6 18.8 %collective-permute-start.8 = (f32[2,32,1,128]{3,2,1,0:T(1,128)S(1)}, f32[2,32,1,128]{3,2,1,0:T(1,128)S(1)}, u32[]{:S(2)}, u32[]{:S(2)}) collective-permute-start(f32[2,32,1,128]{3,2,1,0:T(1,128)S(1)} %slice.115), channel_id=1, source_target_pairs={{1,0},{2,1},{3,2},{4,3},{5,4},{6,5},{7,6},{8,7},{9,8},{10,9},{11,1... | collective-permute-start | bytes 98312 | tf_op jit(solution)/shard_map/ppermute | solution.py:17
  255.2 16.2 %collective-permute-start.6 = (f32[2,32,16,1]{3,2,1,0:T(8,128)S(1)}, f32[2,32,16,1]{3,2,1,0:T(8,128)S(1)}, u32[]{:S(2)}, u32[]{:S(2)}) collective-permute-start(f32[2,32,16,1]{3,2,1,0:T(8,128)S(1)} %bitcast.8), channel_id=1, source_target_pairs={{0,496},{16,0},{32,16},{48,32},{64,48},{80,64},{96,80},{112,96},{1... | collective-permute-start | bytes 12296 | tf_op jit(solution)/shard_map/ppermute | solution.py:11
  271.8 21.4 %collective-permute-start.9 = (f32[2,32,1,128]{3,2,1,0:T(1,128)S(1)}, f32[2,32,1,128]{3,2,1,0:T(1,128)S(1)}, u32[]{:S(2)}, u32[]{:S(2)}) collective-permute-start(f32[2,32,1,128]{3,2,1,0:T(1,128)S(1)} %slice.116), channel_id=1, source_target_pairs={{0,1},{1,2},{2,3},{3,4},{4,5},{5,6},{6,7},{7,8},{8,9},{9,10},{10,1... | collective-permute-start | bytes 98312 | tf_op jit(solution)/shard_map/ppermute | solution.py:17
  274.5 18.7 %collective-permute-start.7 = (f32[2,32,16,1]{3,2,1,0:T(8,128)S(1)}, f32[2,32,16,1]{3,2,1,0:T(8,128)S(1)}, u32[]{:S(2)}, u32[]{:S(2)}) collective-permute-start(f32[2,32,16,1]{3,2,1,0:T(8,128)S(1)} %slice.112), channel_id=1, source_target_pairs={{0,16},{16,32},{32,48},{48,64},{64,80},{80,96},{96,112},{112,128},... | collective-permute-start | bytes 12296 | tf_op jit(solution)/shard_map/ppermute | solution.py:11
